TPU v7x, 128 devices: a whole 4x4x4 slice. The times are simulated.
128 devices in a mesh: tp: 4 (over z_lo, core), ep: 32 (over y, x, z_hi).
Axes of the slice: x: 4, y: 4, z: 4 (z_hi: 2, z_lo: 2; z = z_hi * 2 + z_lo), core: 2. Of those that a mesh axis runs over, the one named last changes fastest.
Arguments:
- hidden_in: bfloat16 [4096, 7168], P('ep', 'tp'), may hold values from -6 to 6
- next_ids: int32 [4096], P('ep'), may hold values from 0 to 65535, as said below
- embed_table: bfloat16 [65536, 7168], P('ep', 'tp'), may hold values from -6 to 6
- hidden_gain: float32 [7168], replicated, may hold values from 0.5 to 1.5
- embed_gain: float32 [7168], replicated, may hold values from 0.5 to 1.5
- ffn_gain: float32 [7168], P('tp'), may hold values from 0.5 to 1.5
- proj_weight: bfloat16 [2, 7168, 7168], P(None, 'ep', 'tp'), may hold values from -0.046875 to 0.046875
- routes: int32 [4096, 8], P('ep'), may hold values from 0 to 31, all different within a row; in each aligned block of 128 rows (0 to 127, 128 to 255, ...) at most 40 rows name the same one
- route_weights: float32 [4096, 8], P('ep'), may hold values from 0.05 to 0.5
- w_gate_up: bfloat16 [32, 7168, 2, 1024], P('ep', 'tp'), may hold values from -0.0625 to 0.0625
- w_down: bfloat16 [32, 1024, 7168], P('ep', None, 'tp'), may hold values from -0.1875 to 0.1875
- shared_gate_up: bfloat16 [7168, 2, 1024], P(('tp', 'ep')), may hold values from -0.0625 to 0.0625
- shared_down: bfloat16 [1024, 7168], P('ep', 'tp'), may hold values from -0.1875 to 0.1875
Outputs:
- module_out: bfloat16 [4096, 7168], P('ep', 'tp')
Inputs may be any that keep to these rules, and one draw needn't show every extreme that they name: `routes`: each row names 8 different experts. Among the 128 rows of one index of ep no expert is named by more than 40 rows, and in some of them one expert is named by exactly 40. `next_ids`: vocabulary row v lies with index v // 2048 of ep. Among the 128 tokens of one index of ep at most 8 have their next token with one such index, and in every index of ep one is reached by exactly 8.
All inputs are finite; a program needn't handle non-finite values.
Results may differ from a plain program's by a relative error of at most 0.03.
Values may be sent and summed in bfloat16 or wider, within the bound.
No kernel may reach another device: no remote copies, remote signals or barrier semaphores. Data moves between devices by JAX's collectives and lax.ppermute only.
A program may use at most 128 MiB of HBM per device.

v0:
```python
import jax
import jax.numpy as jnp
from jax import lax
from jax.sharding import Mesh
from jax.sharding import PartitionSpec as P

EP = ("ep_0", "ep_1", "ep_2")
TP_EP = ("tp", "ep_0", "ep_1", "ep_2")


def own_rows(terms, axes):
    total = terms.astype(jnp.bfloat16)
    for axis in axes:
        total = lax.psum_scatter(total, axis, scatter_dimension=0, tiled=True)
    return total.astype(jnp.float32)


def copy_for_each(shard, axis):
    copies = jnp.broadcast_to(shard, (lax.axis_size(axis), *shard.shape))
    return lax.all_to_all(copies, axis, split_axis=0, concat_axis=0, tiled=True)


def over_copies(shard, axis):
    return copy_for_each(shard, axis).sum(axis=0)


def joined_along(blocks, dim):
    blocks = jnp.moveaxis(blocks, 0, dim)
    dims = blocks.shape
    return blocks.reshape(*dims[:dim], dims[dim] * dims[dim + 1], *dims[dim + 2 :])


def gathered_copies(shard, axis, dim):
    blocks = copy_for_each(shard, axis)
    return joined_along(blocks, dim)


def split_up(shard, dim, length):
    before, after = (shard.shape[:dim], shard.shape[dim + 1 :])
    return jnp.moveaxis(shard.reshape(*before, length, -1, *after), dim, 0)


def sum_at_owner(shard, axis, dim):
    blocks = split_up(shard, dim, lax.axis_size(axis))
    arrived = lax.all_to_all(blocks, axis, split_axis=0, concat_axis=0, tiled=True)
    return arrived.astype(jnp.float32).sum(axis=0)


def rms_norm(values, gain):
    values = values.astype(jnp.float32)
    scale = lax.rsqrt(jnp.mean(values * values, axis=-1, keepdims=True) + 1e-06)
    return (values * scale * gain).astype(jnp.bfloat16)


def gated(pair):
    return (jax.nn.silu(pair[:, 0]) * pair[:, 1]).astype(jnp.bfloat16)


def on_device(
    hidden_in,
    next_ids,
    embed_table,
    hidden_gain,
    embed_gain,
    ffn_gain,
    proj_weight,
    routes,
    route_weights,
    w_gate_up,
    w_down,
    shared_gate_up,
    shared_down,
):
    tok_rows = hidden_in.shape[0]
    local_width = hidden_in.shape[1]
    ep_count = lax.axis_size(EP)
    tp_count = lax.axis_size("tp")
    vocab_rows = embed_table.shape[0]
    id_slots = max(2, 2 * tok_rows // ep_count)
    holder = next_ids // vocab_rows
    marks = (holder[:, None] == jnp.arange(ep_count, dtype=jnp.int32)[None, :]).astype(jnp.int32)
    before = jnp.cumsum(marks, axis=0) - marks
    order = jnp.sum(before * marks, axis=1)
    id_place = holder * id_slots + order
    asked = (
        jnp.zeros((ep_count * id_slots,), jnp.int32)
        .at[id_place]
        .set(next_ids - holder * vocab_rows + 1)
    )
    asked = asked.reshape(ep_count, id_slots)
    arrived_ids = lax.all_to_all(asked, EP, split_axis=0, concat_axis=0, tiled=True)
    found = jnp.take(embed_table, jnp.maximum(arrived_ids - 1, 0).reshape(-1), axis=0)
    found = found.reshape(arrived_ids.shape[0], arrived_ids.shape[1], -1)
    answered = lax.all_to_all(found, EP, split_axis=0, concat_axis=0, tiled=True)
    embedded = jnp.take(answered.reshape(ep_count * id_slots, local_width), id_place, axis=0)
    part_hidden, part_embed = (
        lax.all_to_all(hidden_in, "tp", split_axis=0, concat_axis=1, tiled=True),
        lax.all_to_all(embedded, "tp", split_axis=0, concat_axis=1, tiled=True),
    )
    joined = jnp.stack(
        [rms_norm(part_hidden, hidden_gain), rms_norm(part_embed, embed_gain)], axis=1
    )
    spread = lax.all_to_all(joined, EP, split_axis=2, concat_axis=0, tiled=True)
    whole = lax.all_gather(spread, "tp", axis=0, tiled=True)
    layout = whole.reshape(tp_count, ep_count, tok_rows // tp_count, -1)
    weight_block = proj_weight.reshape(-1, proj_weight.shape[2])
    projected = own_rows(
        jnp.dot(
            layout.transpose(1, 0, 2, 3).reshape(tok_rows * lax.axis_size(EP), -1),
            weight_block,
            preferred_element_type=jnp.float32,
        ),
        EP,
    ).astype(jnp.bfloat16)
    residual_rows = projected.astype(jnp.float32)
    squares = over_copies(jnp.sum(residual_rows * residual_rows, axis=1), "tp")
    model_width = local_width * tp_count
    normed = (residual_rows * lax.rsqrt(squares / model_width + 1e-06)[:, None] * ffn_gain).astype(
        jnp.bfloat16
    )
    top_count = routes.shape[1]
    capacity = min(tok_rows, tok_rows * top_count * 5 // (4 * ep_count))
    chosen = routes.reshape(-1)
    hits = (chosen[:, None] == jnp.arange(ep_count, dtype=jnp.int32)[None, :]).astype(jnp.int32)
    earlier = jnp.cumsum(hits, axis=0) - hits
    rank = jnp.sum(earlier * hits, axis=1)
    slot = chosen * capacity + rank
    owner_token = jnp.arange(tok_rows * top_count, dtype=jnp.int32) // top_count + 1
    source = jnp.zeros((ep_count * capacity,), jnp.int32).at[slot].set(owner_token)
    filled = source > 0
    outgoing = jnp.where(
        filled[:, None],
        jnp.take(normed, jnp.maximum(source - 1, 0), axis=0),
        jnp.zeros((), jnp.bfloat16),
    )
    outgoing = outgoing.reshape(ep_count, capacity, local_width)
    gate_up_block = w_gate_up.reshape(w_gate_up.shape[1], -1)
    down_block = w_down.reshape(w_down.shape[1], w_down.shape[2])
    expert_width = w_gate_up.shape[3]
    arrived = lax.all_to_all(outgoing, EP, split_axis=0, concat_axis=0, tiled=True)
    slots = arrived.shape[1]
    rows = arrived.reshape(-1, arrived.shape[2])
    pair = jnp.dot(rows, gate_up_block, preferred_element_type=jnp.float32).reshape(
        -1, 2, expert_width
    )
    share = lax.psum_scatter(
        pair.astype(jnp.bfloat16), "tp", scatter_dimension=2, tiled=True
    ).astype(jnp.float32)
    act = gathered_copies(gated(share), "tp", 1)
    result = jnp.dot(act, down_block, preferred_element_type=jnp.float32).astype(jnp.bfloat16)
    returned = lax.all_to_all(
        result.reshape(ep_count, slots, -1), EP, split_axis=0, concat_axis=0, tiled=True
    )
    shared_width = shared_gate_up.shape[2]
    piece = lax.all_gather(shared_gate_up, EP, axis=0, tiled=True)
    columns = normed
    shared_pair = jnp.dot(
        columns, piece.reshape(piece.shape[0], -1), preferred_element_type=jnp.float32
    )
    shared_pair = shared_pair.reshape(tok_rows, 2, shared_width)
    shared_part = sum_at_owner(shared_pair.astype(jnp.bfloat16), "tp", 2)
    shared_act = gathered_copies(gated(shared_part), "tp", 1)
    columns = shared_act
    shared = jnp.dot(
        columns,
        lax.all_gather(shared_down, EP, axis=0, tiled=True),
        preferred_element_type=jnp.float32,
    )
    back_rows = returned.reshape(ep_count * capacity, local_width)
    picked = (
        jnp.take(back_rows, slot, axis=0)
        .astype(jnp.float32)
        .reshape(tok_rows, top_count, local_width)
    )
    routed = jnp.sum(picked * route_weights[:, :, None], axis=1)
    return (residual_rows + routed + shared).astype(jnp.bfloat16)


def solution(mesh):
    finer = Mesh(mesh.devices.reshape(mesh.shape["tp"], 4, 4, 2), ("tp", "ep_0", "ep_1", "ep_2"))
    in_specs = (
        P(EP, "tp"),
        P(EP),
        P(EP, "tp"),
        P(),
        P(),
        P("tp"),
        P(None, EP, "tp"),
        P(EP, None),
        P(EP, None),
        P(EP, "tp", None, None),
        P(EP, None, "tp"),
        P(TP_EP, None, None),
        P(EP, "tp"),
    )
    out_specs = P(EP, "tp")
    return jax.shard_map(
        on_device, mesh=finer, in_specs=in_specs, out_specs=out_specs, check_vma=False
    )
```

profile of v0, /device:TPU:111, one launch (start us, length us, event | category | flops | bytes accessed | tf_op | source)
XLA Modules:
  0.0 791.3 jit_solution(6536944026402755564)
XLA Ops:
  9.7 13.0 %all_to_all.86 = s32[32,1,8]{2,1,0:T(1,128)S(1)} all-to-all(s32[32,1,8]{2,1,0:T(1,128)S(1)} %bitcast.132), channel_id=1, replica_groups=mesh['tp'=4,'ep_0'=4,'ep_1'=4,'ep_2'=2] {'ep_0','ep_1','ep_2'}, dimensions={0} | all-to-all | bytes 2048 | tf_op jit(solution)/shard_map/all_to_all | solution.py:91
  35.8 9.2 %all-to-all-start.2 = ((bf16[32,8,1792]{2,1,0:T(8,128)(2,1)}), bf16[32,8,1792]{2,1,0:T(8,128)(2,1)S(1)}, u32[]{:S(2)}, u32[]{:S(2)}) async-start(bf16[32,8,1792]{2,1,0:T(8,128)(2,1)} %bitcast_select_fusion.1), calls=%async_computation.2 | async-start | bytes 1835008 | tf_op jit(solution)/shard_map/all_to_all | solution.py:94
  49.4 8.5 %all-to-all-done.2 = bf16[32,8,1792]{2,1,0:T(8,128)(2,1)S(1)} async-done(((bf16[32,8,1792]{2,1,0:T(8,128)(2,1)}), bf16[32,8,1792]{2,1,0:T(8,128)(2,1)S(1)}, u32[]{:S(2)}, u32[]{:S(2)}) %all-to-all-start.2) | async-done | bytes 917536 | tf_op jit(solution)/shard_map/all_to_all | solution.py:94
  85.6 20.5 %all_to_all.87 = bf16[32,2,7168]{2,1,0:T(2,128)(2,1)S(1)} all-to-all(bf16[32,2,7168]{2,1,0:T(2,128)(2,1)S(1)} %reshape.399), channel_id=1, replica_groups=mesh['tp'=4,'ep_0'=4,'ep_1'=4,'ep_2'=2] {'ep_0','ep_1','ep_2'}, dimensions={0} | all-to-all | bytes 1835008 | tf_op jit(solution)/shard_map/all_to_all | solution.py:103
  109.3 7.8 copy.127
  117.4 47.3 %all-gather.4.cloned.1.call-done = bf16[4096,2,224]{2,0,1:T(8,128)(2,1)} async-done(((bf16[1024,2,224]{2,0,1:T(8,128)(2,1)}), bf16[4096,2,224]{2,0,1:T(8,128)(2,1)}) %all-gather.4.cloned.1.call-update) | async-done | bytes 3670032 | tf_op jit(solution)/shard_map/all_gather | solution.py:104
  164.7 10.1 %copy.128 = bf16[4096,2,224]{2,1,0:T(2,128)(2,1)} copy(bf16[4096,2,224]{2,0,1:T(8,128)(2,1)} %all-gather.4.cloned.1.call-done) | data formatting | bytes 7340032 | tf_op jit(solution)/shard_map/all_gather | solution.py:104
  185.0 10.4 %convolution_convert_fusion = bf16[4096,1792]{1,0:T(8,128)(2,1)} fusion(bf16[4096,448]{1,0:T(8,128)(2,1)S(1)} %bitcast.125, bf16[448,1792]{1,0:T(8,128)(2,1)S(1)} %bitcast.115), kind=kOutput, calls=%fused_computation.6 | convolution fusion | flops 6584008704 | bytes 19955712 | tf_op jit(solution)/shard_map/dot_general | solution.py:108
  195.5 131.5 %reduce-scatter.5.cloned.1.call-done = bf16[1024,1792]{1,0:T(8,128)(2,1)} async-done(((bf16[4096,1792]{1,0:T(8,128)(2,1)}), bf16[1024,1792]{1,0:T(8,128)(2,1)}) %reduce-scatter.5.cloned.1.call-update) | async-done | bytes 3670032 | tf_op jit(solution)/shard_map/reduce_scatter | solution.py:14
  327.1 44.1 %reduce-scatter.7.cloned.1.call-done = bf16[256,1792]{1,0:T(8,128)(2,1)} async-done(((bf16[1024,1792]{1,0:T(8,128)(2,1)}), bf16[256,1792]{1,0:T(8,128)(2,1)}) %reduce-scatter.7.cloned.1.call-update) | async-done | bytes 917520 | tf_op jit(solution)/shard_map/reduce_scatter | solution.py:14
  371.5 9.0 %reduce-window.6 = s32[32,8,128]{2,1,0:T(8,128)S(1)} reduce-window(s32[32,8,128]{2,1,0:T(8,128)S(1)} %fusion.20, s32[]{:T(128)} %constant.119.clone.1), window={size=1x1x128 pad=0_0x0_0x127_0}, to_apply=%region_8.9 | reduce-window | flops 4161536 | bytes 262148 | tf_op jit(solution)/shard_map/reduce-window
  385.6 10.6 %reduce-scatter.9.cloned.1.call-done = bf16[128,1792]{1,0:T(8,128)(2,1)} async-done(((bf16[256,1792]{1,0:T(8,128)(2,1)}), bf16[128,1792]{1,0:T(8,128)(2,1)}) %reduce-scatter.9.cloned.1.call-update) | async-done | bytes 458768 | tf_op jit(solution)/shard_map/reduce_scatter | solution.py:14
  414.3 9.8 %all-to-all-start.6 = ((bf16[32,40,1792]{2,1,0:T(8,128)(2,1)}), bf16[32,40,1792]{2,1,0:T(8,128)(2,1)}, u32[]{:S(2)}, u32[]{:S(2)}) async-start(bf16[32,40,1792]{2,1,0:T(8,128)(2,1)} %select_select_fusion), calls=%async_computation.9 | async-start | bytes 9175040 | tf_op jit(solution)/shard_map/all_to_all | solution.py:140
  424.4 9.2 %copy.151 = bf16[224,8,2,1024]{3,1,2,0:T(8,128)(2,1)} copy(bf16[224,8,2,1024]{3,2,1,0:T(2,128)(2,1)} %bitcast.122) | data formatting | bytes 14680064
  433.6 10.1 %copy.138 = bf16[2048,1792]{1,0:T(8,128)(2,1)} copy(bf16[2048,1792]{0,1:T(8,128)(2,1)} %bitcast.116) | data formatting | bytes 14680064 | tf_op jit(solution)/shard_map/dot_general | solution.py:143
  443.7 46.4 %all-to-all-done.6 = bf16[32,40,1792]{2,1,0:T(8,128)(2,1)} async-done(((bf16[32,40,1792]{2,1,0:T(8,128)(2,1)}), bf16[32,40,1792]{2,1,0:T(8,128)(2,1)}, u32[]{:S(2)}, u32[]{:S(2)}) %all-to-all-start.6) | async-done | bytes 4587552 | tf_op jit(solution)/shard_map/all_to_all | solution.py:140
  490.1 14.9 %convolution_convert_fusion.2 = bf16[1280,2,1024]{2,0,1:T(8,128)(2,1)} fusion(bf16[1280,1792,1]{1,0,2:T(8,128)(2,1)} %bitcast.21, bf16[2,1024,1792]{2,1,0:T(8,128)(2,1)} %bitcast.123), kind=kOutput, calls=%fused_computation.11 | convolution fusion | flops 9397862400 | bytes 17170432 | tf_op jit(solution)/shard_map/dot_general | solution.py:143
  505.6 56.3 %reduce-scatter.11.cloned.1.call-done = bf16[1280,2,256]{2,0,1:T(8,128)(2,1)} async-done(((bf16[1280,2,1024]{2,0,1:T(8,128)(2,1)}), bf16[1280,2,256]{2,0,1:T(8,128)(2,1)}) %reduce-scatter.11.cloned.1.call-update) | async-done | bytes 1310736 | tf_op jit(solution)/shard_map/reduce_scatter | solution.py:146
  571.8 66.9 %all-gather.6.cloned.1.call-done = bf16[1792,2,1024]{2,1,0:T(2,128)(2,1)} async-done(((bf16[56,2,1024]{2,1,0:T(2,128)(2,1)}), bf16[1792,2,1024]{2,1,0:T(2,128)(2,1)}) %all-gather.6.cloned.1.call-update) | async-done | bytes 7340048 | tf_op jit(solution)/shard_map/all_gather | solution.py:155
  638.7 18.7 %copy.145 = bf16[1792,2,1024]{0,2,1:T(8,128)(2,1)} copy(bf16[1792,2,1024]{2,1,0:T(2,128)(2,1)} %all-gather.6.cloned.1.call-done) | data formatting | bytes 14680064 | tf_op jit(solution)/shard_map/reshape | solution.py:158
  668.1 9.9 %convolution_convert_fusion.1 = bf16[1280,1792]{1,0:T(8,128)(2,1)} fusion(bf16[1280,1024]{0,1:T(8,128)(2,1)} %bitcast.27, bf16[1,1024,1792]{2,1,0:T(8,128)(2,1)} %param.23), kind=kOutput, calls=%fused_computation.7 | convolution fusion | flops 4699914240 | bytes 10878976 | tf_op jit(solution)/shard_map/dot_general | solution.py:150
  677.9 9.9 %all-to-all-start.8 = ((bf16[32,40,1792]{2,1,0:T(8,128)(2,1)}), bf16[32,40,1792]{2,1,0:T(8,128)(2,1)}, u32[]{:S(2)}, u32[]{:S(2)}) async-start(bf16[32,40,1792]{2,1,0:T(8,128)(2,1)} %bitcast.124), calls=%async_computation.12 | async-start | bytes 9175040 | tf_op jit(solution)/shard_map/all_to_all | solution.py:151
  688.5 68.2 %all-to-all-done.8 = bf16[32,40,1792]{2,1,0:T(8,128)(2,1)} async-done(((bf16[32,40,1792]{2,1,0:T(8,128)(2,1)}), bf16[32,40,1792]{2,1,0:T(8,128)(2,1)}, u32[]{:S(2)}, u32[]{:S(2)}) %all-to-all-start.8) | async-done | bytes 4587552 | tf_op jit(solution)/shard_map/all_to_all | solution.py:151
  764.5 10.9 %gather_fusion.3 = bf16[1024,1792]{1,0:T(8,128)(2,1)} fusion(bf16[1280,1792]{1,0:T(8,128)(2,1)} %bitcast.30, s32[1024]{0:T(1024)S(1)} %broadcast_clamp_fusion), kind=kCustom, calls=%fused_computation.3 | custom fusion | bytes 7344128 | tf_op jit(solution)/shard_map/jit(_take)/gather | solution.py:171
  (127 shorter events, 122.5 us)
Async XLA Ops:
  7.4 177.6 %copy-start = (bf16[2,224,1792]{2,1,0:T(8,128)(2,1)S(1)}, bf16[2,224,1792]{2,1,0:T(8,128)(2,1)}, u32[]{:S(2)}) copy-start(bf16[2,224,1792]{2,1,0:T(8,128)(2,1)} %param.19) | copy-start | bytes 4816900
  22.7 13.2 %all-to-all-start = ((bf16[4,32,1792]{2,1,0:T(8,128)(2,1)}), bf16[4,32,1792]{2,1,0:T(8,128)(2,1)S(1)}, u32[]{:S(2)}, u32[]{:S(2)}) async-start(bf16[4,32,1792]{2,1,0:T(8,128)(2,1)} %bitcast.131), calls=%async_computation | async-start | bytes 917504 | tf_op jit(solution)/shard_map/all_to_all | solution.py:97
  35.8 22.0 %all-to-all-start.2 = ((bf16[32,8,1792]{2,1,0:T(8,128)(2,1)}), bf16[32,8,1792]{2,1,0:T(8,128)(2,1)S(1)}, u32[]{:S(2)}, u32[]{:S(2)}) async-start(bf16[32,8,1792]{2,1,0:T(8,128)(2,1)} %bitcast_select_fusion.1), calls=%async_computation.2 | async-start | bytes 1835008 | tf_op jit(solution)/shard_map/all_to_all | solution.py:94
  58.8 13.9 %copy-start.4 = (f32[7168]{0:T(1024)S(1)}, f32[7168]{0:T(1024)}, u32[]{:S(2)}) copy-start(f32[7168]{0:T(1024)} %param.17) | copy-start | bytes 86020
  58.8 13.9 %copy-start.5 = (f32[7168]{0:T(1024)S(1)}, f32[7168]{0:T(1024)}, u32[]{:S(2)}) copy-start(f32[7168]{0:T(1024)} %param.16) | copy-start | bytes 86020
  59.7 10.7 %all-to-all-start.3 = ((bf16[4,32,1792]{2,1,0:T(8,128)(2,1)}), bf16[4,32,1792]{2,1,0:T(8,128)(2,1)S(1)}, u32[]{:S(2)}, u32[]{:S(2)}) async-start(bf16[4,32,1792]{2,1,0:T(8,128)(2,1)} %broadcast_select_fusion), calls=%async_computation.3 | async-start | bytes 917504 | tf_op jit(solution)/shard_map/all_to_all | solution.py:98
  64.1 100.6 %all-gather.4.cloned.1.call-start = ((), (), s32[]{:S(2)}) async-start(), calls=%async_computation.15 | async-start | bytes 5242880 | tf_op jit(solution)/shard_map/all_gather | solution.py:104
  117.2 209.8 %reduce-scatter.5.cloned.1.call-start = ((), (), s32[]{:S(2)}) async-start(), calls=%async_computation.16 | async-start | bytes 18350080 | tf_op jit(solution)/shard_map/reduce_scatter | solution.py:14
  195.5 175.8 %copy-start.3 = (s32[128,8]{0,1:T(8,128)S(1)}, s32[128,8]{0,1:T(8,128)}, u32[]{:S(2)}) copy-start(s32[128,8]{0,1:T(8,128)} %param.20) | copy-start | bytes 12292
  195.5 207.7 %copy-start.6 = (f32[1792]{0:T(1024)S(1)}, f32[1792]{0:T(1024)}, u32[]{:S(2)}) copy-start(f32[1792]{0:T(1024)} %param.18) | copy-start | bytes 21508
  195.5 175.7 %reduce-scatter.7.cloned.1.call-start = ((), (), s32[]{:S(2)}) async-start(), calls=%async_computation.17 | async-start | bytes 4587520 | tf_op jit(solution)/shard_map/reduce_scatter | solution.py:14
  327.1 69.2 %reduce-scatter.9.cloned.1.call-start = ((), (), s32[]{:S(2)}) async-start(), calls=%async_computation.18 | async-start | bytes 1376256 | tf_op jit(solution)/shard_map/reduce_scatter | solution.py:14
  398.0 5.1 all-to-all-start.5
  414.3 75.8 %all-to-all-start.6 = ((bf16[32,40,1792]{2,1,0:T(8,128)(2,1)}), bf16[32,40,1792]{2,1,0:T(8,128)(2,1)}, u32[]{:S(2)}, u32[]{:S(2)}) async-start(bf16[32,40,1792]{2,1,0:T(8,128)(2,1)} %select_select_fusion), calls=%async_computation.9 | async-start | bytes 9175040 | tf_op jit(solution)/shard_map/all_to_all | solution.py:140
  424.2 137.8 %reduce-scatter.11.cloned.1.call-start = ((), (), s32[]{:S(2)}) async-start(), calls=%async_computation.19 | async-start | bytes 6553600 | tf_op jit(solution)/shard_map/reduce_scatter | solution.py:146
  505.1 133.6 %all-gather.6.cloned.1.call-start = ((), (), s32[]{:S(2)}) async-start(), calls=%async_computation.20 | async-start | bytes 7569408 | tf_op jit(solution)/shard_map/all_gather | solution.py:155
  565.8 98.0 %all-to-all-start.7 = ((bf16[4,1280,256]{1,2,0:T(8,128)(2,1)}), bf16[4,1280,256]{1,2,0:T(8,128)(2,1)}, u32[]{:S(2)}, u32[]{:S(2)}) async-start(bf16[4,1280,256]{1,2,0:T(8,128)(2,1)} %broadcast_in_dim.106), calls=%async_computation.11 | async-start | bytes 5242880 | tf_op jit(solution)/shard_map/all_to_all | solution.py:20
  571.2 209.1 %all-gather.8.cloned.1.call-start = ((), (), s32[]{:S(2)}) async-start(), calls=%async_computation.21 | async-start | bytes 3784704 | tf_op jit(solution)/shard_map/all_gather | solution.py:166
  663.8 14.1 %all-to-all-start.9 = ((bf16[4,128,2,256]{3,1,2,0:T(8,128)(2,1)}), bf16[4,128,2,256]{3,1,2,0:T(8,128)(2,1)S(1)}, u32[]{:S(2)}, u32[]{:S(2)}) async-start(bf16[4,128,2,256]{3,1,2,0:T(8,128)(2,1)} %bitcast.114), calls=%async_computation.13 | async-start | bytes 1048576 | tf_op jit(solution)/shard_map/all_to_all | solution.py:45
  677.9 10.2 %copy-start.7 = (f32[128,8]{0,1:T(8,128)S(1)}, f32[128,8]{0,1:T(8,128)}, u32[]{:S(2)}) copy-start(f32[128,8]{0,1:T(8,128)} %param.21) | copy-start | bytes 12292
  677.9 78.8 %all-to-all-start.8 = ((bf16[32,40,1792]{2,1,0:T(8,128)(2,1)}), bf16[32,40,1792]{2,1,0:T(8,128)(2,1)}, u32[]{:S(2)}, u32[]{:S(2)}) async-start(bf16[32,40,1792]{2,1,0:T(8,128)(2,1)} %bitcast.124), calls=%async_computation.12 | async-start | bytes 9175040 | tf_op jit(solution)/shard_map/all_to_all | solution.py:151
  757.4 22.8 %all-to-all-start.10 = ((bf16[4,128,256]{1,2,0:T(8,128)(2,1)}), bf16[4,128,256]{1,2,0:T(8,128)(2,1)S(1)}, u32[]{:S(2)}, u32[]{:S(2)}) async-start(bf16[4,128,256]{1,2,0:T(8,128)(2,1)} %broadcast_in_dim.108), calls=%async_computation.14 | async-start | bytes 524288 | tf_op jit(solution)/shard_map/all_to_all | solution.py:20
  764.5 19.2 %copy-start.1 = (bf16[2,224,1792]{2,1,0:T(8,128)(2,1)S(1)}, bf16[2,224,1792]{2,1,0:T(8,128)(2,1)}, u32[]{:S(2)}) copy-start(bf16[2,224,1792]{2,1,0:T(8,128)(2,1)} %param.19) | copy-start | bytes 4816900
  775.5 4.8 copy-start.2
Sparse Core Ops, SparseCore 0:
  117.3 47.3 all-gather.3
  195.6 131.4 reduce-scatter.4
  329.5 41.6 reduce-scatter.6
  373.4 22.7 reduce-scatter.8
  505.2 56.6 reduce-scatter.10
Sparse Core Ops, SparseCore 1:
  508.5 130.1 all-gather.5
  641.5 116.5 all-gather.7
where the time goes:
time: 802 us; the launch traced here: 791 us
  waiting for transfers between devices  488 us (61%)
  local copies, waits for them, and re-layouts  122 us (15%)
  starting transfers between devices  60 us (7%)
  matrix products  44.3 us (6%)
  blocking collectives  33.5 us (4%)
  other arithmetic  28.2 us (4%)
  between operations  15.4 us (2%)
    reduce_scatter x3, waiting for transfers between devices, own_rows(): total = lax.psum_scatter(total, axis, scatter_dimension=0, tiled=True)  186 us
    all_to_all x1, waiting for transfers between devices, on_device(): lax.all_to_all(result.reshape(ep_count, slots, -1), EP, split_axis=0, con...  68.2 us
    all_gather x1, waiting for transfers between devices, on_device(): piece = lax.all_gather(shared_gate_up, EP, axis=0, tiled=True)  66.9 us
    reduce_scatter x1, waiting for transfers between devices, on_device(): lax.psum_scatter(pair.astype(jnp.bfloat16), 'tp', scatter_dimension=2, ti...  56.3 us
    all_gather x1, waiting for transfers between devices, on_device(): whole = lax.all_gather(spread, 'tp', axis=0, tiled=True)  47.3 us
    all_to_all x1, waiting for transfers between devices, on_device(): lax.all_to_all(outgoing, EP, split_axis=0, concat_axis=0, tiled=True)  46.4 us
    all_to_all x1, blocking collectives, on_device(): spread = lax.all_to_all(joined, EP, split_axis=2, concat_axis=0, tiled=True)  20.5 us
    reshape x1, local copies, waits for them, and re-layouts, on_device(): piece.reshape(piece.shape[0], -1)  18.7 us
  transfers between devices with their start and end apart: 16, of which 11 were waited for; matrix products, arithmetic and copies ran while one was open for 13% of the time, Pallas kernels for 0%

commit v1 on v0

v1 whole, which is shorter than its diff:
```python
import jax
import jax.numpy as jnp
from jax import lax
from jax.experimental import pallas as pl
from jax.experimental.pallas import tpu as pltpu
from jax.sharding import Mesh
from jax.sharding import PartitionSpec as P

EP = ("ep_0", "ep_1", "ep_2")
XZ = ("ep_1", "ep_2")
TP_EP = ("tp", "ep_0", "ep_1", "ep_2")
BF = jnp.bfloat16
F32 = jnp.float32


def params(*semantics):
    return pltpu.CompilerParams(dimension_semantics=semantics)


def cost(flops, moved):
    return pl.CostEstimate(flops=int(flops), bytes_accessed=int(moved), transcendentals=0)


def swap(value, bit):
    return lax.ppermute(value, "tp", [(i, i ^ bit) for i in range(4)])


def copies(value, axes, count):
    spread = jnp.broadcast_to(value[None], (count, *value.shape))
    return lax.all_to_all(spread, axes, split_axis=0, concat_axis=0, tiled=True)


def feature_blocks(rows, scale, gain, count):
    n, width = rows.shape
    part = width // count

    def kernel(x_ref, s_ref, g_ref, o_ref):
        v = x_ref[...].astype(F32) * s_ref[...] * g_ref[...]
        for b in range(count):
            o_ref[b] = v[:, b * part : (b + 1) * part].astype(BF)

    return pl.pallas_call(
        kernel,
        out_shape=jax.ShapeDtypeStruct((count, n, part), BF),
        cost_estimate=cost(4 * n * width, 4 * n * width),
    )(rows, scale, gain)


def found_blocks(ids, table, scales, gain, planes, count):
    slots = ids.shape[0]
    vocab, width = table.shape
    part = width // count
    step = 512
    each = slots // planes

    def kernel(i_ref, t_ref, s_ref, g_ref, o_ref, acc, sc):
        k = pl.program_id(0)

        @pl.when(k == 0)
        def _():
            acc[...] = jnp.zeros_like(acc)
            sc[...] = jnp.zeros_like(sc)

        hit = i_ref[:, 0:1] - 1 == lax.broadcasted_iota(jnp.int32, (slots, step), 1) + k * step
        acc[...] += jnp.dot(
            jnp.where(hit, 1.0, 0.0).astype(BF), t_ref[...], preferred_element_type=F32
        )
        sc[...] += jnp.sum(jnp.where(hit, s_ref[...], 0.0), axis=1, keepdims=True)

        @pl.when(k == pl.num_programs(0) - 1)
        def _():
            v = acc[...] * sc[...] * g_ref[...]
            for b in range(count):
                piece = v[:, b * part : (b + 1) * part].astype(BF)
                for y in range(planes):
                    o_ref[y, b] = piece[y * each : (y + 1) * each]

    return pl.pallas_call(
        kernel,
        grid=(vocab // step,),
        in_specs=[
            pl.BlockSpec((slots, ids.shape[1]), lambda k: (0, 0)),
            pl.BlockSpec((step, width), lambda k: (k, 0)),
            pl.BlockSpec((1, step), lambda k: (0, k)),
            pl.BlockSpec((1, width), lambda k: (0, 0)),
        ],
        out_specs=pl.BlockSpec((planes, count, each, part), lambda k: (0, 0, 0, 0)),
        out_shape=jax.ShapeDtypeStruct((planes, count, each, part), BF),
        scratch_shapes=[pltpu.VMEM((slots, width), F32), pltpu.VMEM((slots, 1), F32)],
        compiler_params=params("arbitrary"),
        cost_estimate=cost(2 * slots * vocab * width, 2 * vocab * width),
    )(ids, table, scales, gain)


def picked_blocks(arrived, places, tokens):
    holders, rows, part = arrived.shape
    sources = places.shape[0]
    each = rows // sources
    slots = holders * each

    def kernel(a_ref, p_ref, o_ref):
        hit = lax.broadcasted_iota(jnp.int32, (slots, tokens), 0) == p_ref[0, 0:1, :]
        o_ref[0] = lax.dot_general(
            jnp.where(hit, 1.0, 0.0).astype(BF),
            a_ref[...].reshape(slots, part),
            (((0,), (0,)), ((), ())),
            preferred_element_type=F32,
        ).astype(BF)

    return pl.pallas_call(
        kernel,
        grid=(sources,),
        in_specs=[
            pl.BlockSpec((holders, each, part), lambda s: (0, s, 0)),
            pl.BlockSpec((1, places.shape[1], tokens), lambda s: (s, 0, 0)),
        ],
        out_specs=pl.BlockSpec((1, tokens, part), lambda s: (s, 0, 0)),
        out_shape=jax.ShapeDtypeStruct((sources, tokens, part), BF),
        compiler_params=params("arbitrary"),
        cost_estimate=cost(2 * sources * slots * tokens * part, 4 * holders * rows * part),
    )(arrived, places)


def partial_projection(index, acts, weights, half, start, out_type):
    rows, part = acts[0].shape
    width = weights.shape[3]
    tile = 256

    def kernel(idx, *refs):
        a, w, rest = refs[:4], refs[4:8], refs[8:]
        total = rest[0][...] if start is not None else None
        for q in range(4):
            term = jnp.dot(a[q][...], w[q][0, 0], preferred_element_type=F32)
            total = term if total is None else total + term
        rest[-1][...] = total.astype(out_type)

    def weight_spec(q):
        return pl.BlockSpec((1, 1, part, tile), lambda n, idx: (idx[q], half, 0, n))

    in_specs = [pl.BlockSpec((rows, part), lambda n, idx: (0, 0))] * 4
    in_specs += [weight_spec(q) for q in range(4)]
    operands = [*acts, *([weights] * 4)]
    if start is not None:
        in_specs.append(pl.BlockSpec((rows, tile), lambda n, idx: (0, n)))
        operands.append(start)
    return pl.pallas_call(
        kernel,
        grid_spec=pltpu.PrefetchScalarGridSpec(
            num_scalar_prefetch=1,
            grid=(width // tile,),
            in_specs=in_specs,
            out_specs=pl.BlockSpec((rows, tile), lambda n, idx: (0, n)),
        ),
        out_shape=jax.ShapeDtypeStruct((rows, width), out_type),
        compiler_params=params("arbitrary"),
        cost_estimate=cost(8 * rows * part * width, 6 * rows * width),
    )(index, *operands)


def gained_columns(weights, gain, count):
    depth, _, width = weights.shape
    part = width // count
    step = 256

    def kernel(w_ref, g_ref, o_ref):
        g = g_ref[...]
        o_ref[0, :, 0:part] = (w_ref[:, 0, :].astype(F32) * g).astype(BF)
        o_ref[0, :, part : 2 * part] = (w_ref[:, 1, :].astype(F32) * g).astype(BF)

    return pl.pallas_call(
        kernel,
        grid=(depth // step, count),
        in_specs=[
            pl.BlockSpec((step, 2, part), lambda k, t: (k, 0, t)),
            pl.BlockSpec((step, 1), lambda k, t: (k, 0)),
        ],
        out_specs=pl.BlockSpec((1, step, 2 * part), lambda k, t: (t, k, 0)),
        out_shape=jax.ShapeDtypeStruct((count, depth, 2 * part), BF),
        compiler_params=params("arbitrary", "arbitrary"),
        cost_estimate=cost(2 * depth * width, 8 * depth * width),
    )(weights, gain)


def column_products(index, rows, weights, count):
    n, depth = rows.shape
    part = weights.shape[2]

    def kernel(idx, x_ref, w_ref, o_ref):
        o_ref[0] = jnp.dot(x_ref[...], w_ref[0], preferred_element_type=F32).astype(BF)

    return pl.pallas_call(
        kernel,
        grid_spec=pltpu.PrefetchScalarGridSpec(
            num_scalar_prefetch=1,
            grid=(count,),
            in_specs=[
                pl.BlockSpec((n, depth), lambda b, idx: (0, 0)),
                pl.BlockSpec((1, depth, part), lambda b, idx: (idx[b], 0, 0)),
            ],
            out_specs=pl.BlockSpec((1, n, part), lambda b, idx: (b, 0, 0)),
        ),
        out_shape=jax.ShapeDtypeStruct((count, n, part), BF),
        compiler_params=params("arbitrary"),
        cost_estimate=cost(2 * count * n * depth * part, 2 * n * depth + 2 * count * depth * part),
    )(index, rows, weights)


def down_products(index, acts, weights):
    n, part = acts[0].shape
    width = weights.shape[1]
    tile = 256

    def kernel(idx, *refs):
        a, w, o_ref = refs[:4], refs[4:8], refs[8]
        total = None
        for q in range(4):
            term = jnp.dot(a[q][...], w[q][...], preferred_element_type=F32)
            total = term if total is None else total + term
        o_ref[...] = total.astype(BF)

    def weight_spec(q):
        return pl.BlockSpec((part, tile), lambda j, idx: (idx[q], j))

    return pl.pallas_call(
        kernel,
        grid_spec=pltpu.PrefetchScalarGridSpec(
            num_scalar_prefetch=1,
            grid=(width // tile,),
            in_specs=[pl.BlockSpec((n, part), lambda j, idx: (0, 0))] * 4
            + [weight_spec(q) for q in range(4)],
            out_specs=pl.BlockSpec((n, tile), lambda j, idx: (0, j)),
        ),
        out_shape=jax.ShapeDtypeStruct((n, width), BF),
        compiler_params=params("arbitrary"),
        cost_estimate=cost(8 * n * part * width, 2 * n * width),
    )(index, *acts, *([weights] * 4))


def ranked(marks):
    rows = marks.shape[0]
    below = jnp.tril(jnp.ones((rows, rows), BF), -1)
    return jnp.dot(below, marks.astype(BF), preferred_element_type=F32).astype(jnp.int32)


def on_device(
    hidden_in,
    next_ids,
    embed_table,
    hidden_gain,
    embed_gain,
    ffn_gain,
    proj_weight,
    routes,
    route_weights,
    w_gate_up,
    w_down,
    shared_gate_up,
    shared_down,
):
    tokens, width = hidden_in.shape
    ep = lax.axis_size(EP)
    plane = lax.axis_size(XZ)
    planes = ep // plane
    vocab = embed_table.shape[0]
    model = width * 4
    t = lax.axis_index("tp")
    order_q = jnp.stack([t, t ^ 1, t ^ 2, t ^ 3]).astype(jnp.int32)
    experts = jnp.arange(ep, dtype=jnp.int32)

    id_slots = 2 * tokens // ep
    holder = next_ids // vocab
    marks = holder[:, None] == experts[None, :]
    order = jnp.sum(jnp.where(marks, ranked(marks), 0), axis=1)
    place = holder * id_slots + order
    slot_list = jnp.arange(ep * id_slots, dtype=jnp.int32)
    local_id = next_ids - holder * vocab + 1
    asked = jnp.sum(jnp.where(slot_list[:, None] == place[None, :], local_id[None, :], 0), axis=1)
    asked = jnp.broadcast_to(asked.reshape(ep, id_slots, 1), (ep, id_slots, 128))
    ids = lax.all_to_all(asked, EP, split_axis=0, concat_axis=0, tiled=True)
    places = copies(jnp.broadcast_to(place[None, :], (8, tokens)), XZ, plane)

    wide_hidden = hidden_in.astype(F32)
    wide_table = embed_table.astype(F32)
    squares = jnp.concatenate(
        [jnp.sum(wide_table * wide_table, axis=1), jnp.sum(wide_hidden * wide_hidden, axis=1)]
    )
    squares = copies(squares.reshape(-1, 128), "tp", 4).sum(axis=0).reshape(-1)
    scales = lax.rsqrt(squares / model + 1e-06)
    hidden_gain = lax.dynamic_slice(hidden_gain, (t * width,), (width,))[None, :]
    embed_gain = lax.dynamic_slice(embed_gain, (t * width,), (width,))[None, :]

    weights = lax.all_gather(proj_weight, "ep_0", axis=0)
    piece = lax.all_gather(shared_gate_up, EP, axis=0, tiled=True)
    down = lax.all_gather(shared_down, EP, axis=0, tiled=True)

    def over_tp(blocks):
        own = blocks.reshape(plane * tokens, -1)
        other = swap(own, 2)
        return [own, swap(own, 1), other, swap(other, 1)]

    hidden_blocks = feature_blocks(hidden_in, scales[vocab:, None], hidden_gain, plane)
    hidden_blocks = lax.all_to_all(hidden_blocks, XZ, split_axis=0, concat_axis=0, tiled=True)
    start = partial_projection(order_q, over_tp(hidden_blocks), weights, 0, None, F32)

    found = found_blocks(
        ids.reshape(ep * id_slots, 128), embed_table, scales[None, :vocab], embed_gain, planes, plane
    )
    found = found.reshape(ep, plane * id_slots, -1)
    found = lax.all_to_all(found, EP, split_axis=0, concat_axis=0, tiled=True)
    embed_blocks = picked_blocks(found, places, tokens)
    partial = partial_projection(order_q, over_tp(embed_blocks), weights, 1, start, BF)

    top = routes.shape[1]
    capacity = min(tokens, tokens * top * 5 // (4 * ep))
    named = routes[:, :, None] == experts[None, None, :]
    hits = jnp.any(named, axis=1)
    share = jnp.sum(jnp.where(named, route_weights[:, :, None], 0.0), axis=1)
    rank = jnp.where(hits, ranked(hits), -1)
    taken = rank.T[:, None, :] == jnp.arange(capacity, dtype=jnp.int32)[None, :, None]
    send = taken.astype(BF).reshape(ep * capacity, tokens)
    combine = jnp.where(taken, share.T[:, None, :], 0.0).astype(BF)
    combine = combine.reshape(ep * capacity, tokens)

    partial = lax.all_to_all(
        partial.reshape(plane, tokens, width), XZ, split_axis=0, concat_axis=0, tiled=True
    )
    projected = partial.astype(F32).sum(axis=0).astype(BF)

    outgoing = jnp.dot(send, projected, preferred_element_type=F32).astype(BF)
    arrived = lax.all_to_all(
        outgoing.reshape(ep, capacity, width), EP, split_axis=0, concat_axis=0, tiled=True
    )

    wide = projected.astype(F32)
    squares = copies(jnp.sum(wide * wide, axis=1).reshape(1, tokens), "tp", 4).sum(axis=(0, 1))
    row_scale = lax.rsqrt(squares / model + 1e-06)
    sent_scale = jnp.sum(jnp.where(taken, row_scale[None, None, :], 0.0), axis=2)
    sent_scale = jnp.pad(sent_scale, ((0, 0), (0, 128 - capacity)))[:, None, :]
    slot_scale = lax.all_to_all(sent_scale, EP, split_axis=0, concat_axis=0, tiled=True)
    slot_scale = slot_scale[:, 0, :capacity].reshape(-1, 1)

    def gated(pair, scale):
        hidden = pair.shape[-1] // 2
        pair = pair * scale
        return (jax.nn.silu(pair[:, :hidden]) * pair[:, hidden:]).astype(BF)

    gain_column = ffn_gain[:, None]
    rows = arrived.reshape(ep * capacity, width)
    columns = gained_columns(w_gate_up, gain_column, 4)
    far = column_products(jnp.stack([t ^ 3, t ^ 1]).astype(jnp.int32), rows, columns, 2)
    far = swap(far, 1)
    near = column_products(jnp.stack([t ^ 2, t]).astype(jnp.int32), rows, columns, 2)
    across = swap((far[0].astype(F32) + near[0].astype(F32)).astype(BF), 2)
    pair = far[1].astype(F32) + near[1].astype(F32) + across.astype(F32)
    act = gated(pair, slot_scale)
    other = swap(act, 2)
    acts = [act, swap(act, 1), other, swap(other, 1)]
    down_block = w_down.reshape(w_down.shape[1], w_down.shape[2])
    result = down_products(order_q, acts, down_block)
    returned = lax.all_to_all(
        result.reshape(ep, capacity, width), EP, split_axis=0, concat_axis=0, tiled=True
    )

    shared_columns = gained_columns(piece, gain_column, 4)
    shared_pair = column_products(jnp.arange(4, dtype=jnp.int32), projected, shared_columns, 4)
    shared_pair = lax.all_to_all(shared_pair, "tp", split_axis=0, concat_axis=0, tiled=True)
    shared_act = gated(shared_pair.astype(F32).sum(axis=0), row_scale[:, None])
    shared_act = copies(shared_act, "tp", 4)
    shared_act = shared_act.transpose(1, 0, 2).reshape(tokens, -1)
    shared = jnp.dot(shared_act, down, preferred_element_type=F32)

    routed = lax.dot_general(
        combine,
        returned.reshape(ep * capacity, width),
        (((0,), (0,)), ((), ())),
        preferred_element_type=F32,
    )
    return (projected.astype(F32) + routed + shared).astype(BF)


def solution(mesh):
    finer = Mesh(mesh.devices.reshape(mesh.shape["tp"], 4, 4, 2), ("tp", "ep_0", "ep_1", "ep_2"))
    in_specs = (
        P(EP, "tp"),
        P(EP),
        P(EP, "tp"),
        P(),
        P(),
        P("tp"),
        P(None, EP, "tp"),
        P(EP, None),
        P(EP, None),
        P(EP, "tp", None, None),
        P(EP, None, "tp"),
        P(TP_EP, None, None),
        P(EP, "tp"),
    )
    out_specs = P(EP, "tp")

    def body(*args):
        args = list(args)
        args[9] = args[9].reshape(args[9].shape[1:])
        return on_device(*args)

    return jax.shard_map(body, mesh=finer, in_specs=in_specs, out_specs=out_specs, check_vma=False)
```

time: 802 us -> 528 us (0.66)
  waiting for transfers between devices: 488 us -> 215 us
  Pallas kernels: 0 us -> 115 us
  local copies, waits for them, and re-layouts: 122 us -> 16.5 us
  starting transfers between devices: 60 us -> 103 us
  matrix products: 44.3 us -> 10.5 us
  other arithmetic: 28.2 us -> 16.8 us
    reduce_scatter x4 -> x0, waiting for transfers between devices: 242 us -> none  [the longest x3 186 us: own_rows(): total = lax.psum_scatter(total, axis, scatter_dimension=0, tiled=True)]
    pallas_call x0 -> x11, Pallas kernels: none -> 115 us  [the longest x2 41.2 us: gained_columns(): pl.pallas_call(kernel, grid=(depth // step, count), in_specs=[pl.BlockSpe...]
    all_gather x1, waiting for transfers between devices: 66.9 us -> 0.01 us  [on_device(): piece = lax.all_gather(shared_gate_up, EP, axis=0, tiled=True)]
    all_to_all x9 -> x11, waiting for transfers between devices: 130 us -> 193 us  [the longest x1 68.6 us: on_device(): lax.all_to_all(result.reshape(ep, capacity, width), EP, split_axis=0, con...]
    all_gather x2, waiting for transfers between devices: 47.3 us -> 0.04 us  [the longest x1 0.02 us: on_device(): down = lax.all_gather(shared_down, EP, axis=0, tiled=True)]
    dot_general x5, matrix products: 44.3 us -> 10.5 us  [the longest x1 3.48 us: on_device(): shared = jnp.dot(shared_act, down, preferred_element_type=F32)]
    reshape x4 -> x0, local copies, waits for them, and re-layouts: 27.1 us -> none  [the longest x1 18.7 us: on_device(): piece.reshape(piece.shape[0], -1)]
    gather x4 -> x0, local copies, waits for them, and re-layouts: 23.8 us -> none  [the longest x1 10.9 us: on_device(): jnp.take(back_rows, slot, axis=0).astype(jnp.float32)]
  transfers between devices with their start and end apart: 16 -> 25, of which waited for: 11 -> 9; matrix products, arithmetic and copies ran while one was open for 13% -> 7% of each run, Pallas kernels for 0% -> 22%
where the time goes in v1:
time: 528 us; the launch traced here: 520 us
  waiting for transfers between devices  215 us (41%)
  Pallas kernels  115 us (22%)
  starting transfers between devices  103 us (20%)
  blocking collectives  29.5 us (6%)
  other arithmetic  16.8 us (3%)
  local copies, waits for them, and re-layouts  16.5 us (3%)
  between operations  13.5 us (3%)
  matrix products  10.5 us (2%)
    all_to_all x1, waiting for transfers between devices, on_device(): lax.all_to_all(result.reshape(ep, capacity, width), EP, split_axis=0, con...  68.6 us
    all_to_all x1, waiting for transfers between devices, on_device(): lax.all_to_all(partial.reshape(plane, tokens, width), XZ, split_axis=0, c...  58 us
    all_to_all x1, waiting for transfers between devices, on_device(): lax.all_to_all(outgoing.reshape(ep, capacity, width), EP, split_axis=0, c...  44.7 us
    pallas_call x2, Pallas kernels, gained_columns(): pl.pallas_call(kernel, grid=(depth // step, count), in_specs=[pl.BlockSpe...  41.2 us
    all_to_all x1, blocking collectives, copies(): return lax.all_to_all(spread, axes, split_axis=0, concat_axis=0, tiled=True)  29.5 us
    pallas_call x3, Pallas kernels, column_products(): pl.pallas_call(kernel, grid_spec=pltpu.PrefetchScalarGridSpec(num_scalar_...  25.4 us
    pallas_call x2, Pallas kernels, partial_projection(): pl.pallas_call(kernel, grid_spec=pltpu.PrefetchScalarGridSpec(num_scalar_...  22.5 us
    ppermute x11, waiting for transfers between devices, swap(): return lax.ppermute(value, 'tp', [(i, i ^ bit) for i in range(4)])  20.3 us
  transfers between devices with their start and end apart: 25, of which 9 were waited for; matrix products, arithmetic and copies ran while one was open for 7% of the time, Pallas kernels for 22%

profile of v1, /device:TPU:111, one launch (start us, length us, event | category | flops | bytes accessed | tf_op | source)
XLA Modules:
  0.0 519.9 jit_solution(5256717076355367690)
XLA Ops:
  20.1 6.6 %all-to-all-start.3 = ((s32[8,8,128]{2,1,0:T(8,128)}), s32[8,8,128]{2,1,0:T(8,128)S(1)}, u32[]{:S(2)}, u32[]{:S(2)}) async-start(s32[8,8,128]{2,1,0:T(8,128)} %broadcast_in_dim_broadcast_in_dim_broadcast_in_dim.2), calls=%async_computation.3 | async-start | bytes 65536 | tf_op jit(solution)/shard_map/all_to_all | solution.py:30
  30.3 9.1 %all-to-all-start = ((s32[32,8,128]{2,1,0:T(8,128)}), s32[32,8,128]{2,1,0:T(8,128)S(1)}, u32[]{:S(2)}, u32[]{:S(2)}) async-start(s32[32,8,128]{2,1,0:T(8,128)} %broadcast_in_dim.120), calls=%async_computation | async-start | bytes 262144 | tf_op jit(solution)/shard_map/all_to_all | solution.py:279
  44.3 6.6 %all-to-all-start.4 = ((bf16[8,128,224]{1,2,0:T(8,128)(2,1)}), bf16[8,128,224]{1,2,0:T(8,128)(2,1)S(1)}, u32[]{:S(2)}, u32[]{:S(2)}) async-start(bf16[8,128,224]{1,2,0:T(8,128)(2,1)} %copy.38), calls=%async_computation.4 | async-start | bytes 917504 | tf_op jit(solution)/shard_map/all_to_all | solution.py:302
  52.9 7.0 %shard_map.127 = bf16[4,8,64,224]{3,2,1,0:T(8,128)(2,1)} custom-call(s32[256,128]{1,0:T(8,128)} %bitcast.70, bf16[2048,1792]{1,0:T(8,128)(2,1)} %t_ref.1, f32[1,2048]{1,0:T(1,128)} %bitcast.72, f32[1,1792]{1,0:T(1,128)} %broadcast_in_dim.124.g_ref), custom_call_target="tpu_custom_call" | custom-call | flops 1879048192 | bytes 7340032 | tf_op jit(solution)/shard_map/pallas_call | solution.py:78
  59.9 9.3 %all-to-all-start.2 = ((bf16[32,64,224]{2,1,0:T(8,128)(2,1)}), bf16[32,64,224]{2,1,0:T(8,128)(2,1)S(1)}, u32[]{:S(2)}, u32[]{:S(2)}) async-start(bf16[32,64,224]{2,1,0:T(8,128)(2,1)} %bitcast.62), calls=%async_computation.2 | async-start | bytes 2097152 | tf_op jit(solution)/shard_map/all_to_all | solution.py:309
  71.0 15.2 %all-to-all-done.2.a_ref = bf16[32,64,224]{2,1,0:T(8,128)(2,1)S(1)} async-done(((bf16[32,64,224]{2,1,0:T(8,128)(2,1)}), bf16[32,64,224]{2,1,0:T(8,128)(2,1)S(1)}, u32[]{:S(2)}, u32[]{:S(2)}) %all-to-all-start.2) | async-done | bytes 917536 | tf_op jit(solution)/shard_map/all_to_all | solution.py:309
  96.8 8.5 %collective-permute-done.1.refs_2_ = bf16[1024,224]{1,0:T(8,128)(2,1)S(1)} collective-permute-done((bf16[1024,224]{1,0:T(8,128)(2,1)}, bf16[1024,224]{1,0:T(8,128)(2,1)S(1)}, u32[]{:S(2)}, u32[]{:S(2)}) %collective-permute-start.1) | collective-permute-done | bytes 458784 | tf_op jit(solution)/shard_map/ppermute | solution.py:25
  110.7 10.8 %shard_map.130.refs_8_ = f32[1024,1792]{1,0:T(8,128)} custom-call(s32[4]{0:T(128)} %pad_add_fusion.idx, bf16[1024,224]{1,0:T(8,128)(2,1)} %bitcast.68, bf16[1024,224]{1,0:T(8,128)(2,1)} %copy-done.11, bf16[1024,224]{1,0:T(8,128)(2,1)} %copy-done.8, bf16[1024,224]{1,0:T(8,128)(2,1)} %collective-permute-done.5.refs_3_, bf16[4,2,224,1792]{3,2,1,0:T(8,128)(2,1)} %bitcast.46, ...), custom_call_target="tpu_custom_call" | custom-call | flops 3288334336 | bytes 11010048 | tf_op jit(solution)/shard_map/pallas_call | solution.py:146
  123.0 11.7 %shard_map.131 = bf16[1024,1792]{1,0:T(8,128)(2,1)} custom-call(s32[4]{0:T(128)} %pad_add_fusion.idx, bf16[1024,224]{1,0:T(8,128)(2,1)} %bitcast.65, bf16[1024,224]{1,0:T(8,128)(2,1)} %copy-done.10, bf16[1024,224]{1,0:T(8,128)(2,1)} %copy-done.9, bf16[1024,224]{1,0:T(8,128)(2,1)} %copy-done.12, bf16[4,2,224,1792]{3,2,1,0:T(8,128)(2,1)} %bitcast.50, ...), custom_call_target="tpu_custom_call" | custom-call | flops 3288334336 | bytes 11010048 | tf_op jit(solution)/shard_map/pallas_call | solution.py:146
  134.8 6.5 %all-to-all-start.5 = ((bf16[8,128,1792]{2,1,0:T(8,128)(2,1)}), bf16[8,128,1792]{2,1,0:T(8,128)(2,1)}, u32[]{:S(2)}, u32[]{:S(2)}) async-start(bf16[8,128,1792]{2,1,0:T(8,128)(2,1)} %bitcast.60), calls=%async_computation.5 | async-start | bytes 7340032 | tf_op jit(solution)/shard_map/all_to_all | solution.py:324
  141.8 58.0 %all-to-all-done.5 = bf16[8,128,1792]{2,1,0:T(8,128)(2,1)} async-done(((bf16[8,128,1792]{2,1,0:T(8,128)(2,1)}), bf16[8,128,1792]{2,1,0:T(8,128)(2,1)}, u32[]{:S(2)}, u32[]{:S(2)}) %all-to-all-start.5) | async-done | bytes 3670048 | tf_op jit(solution)/shard_map/all_to_all | solution.py:324
  206.0 8.4 %all-to-all-start.6 = ((bf16[32,40,1792]{2,1,0:T(8,128)(2,1)}), bf16[32,40,1792]{2,1,0:T(8,128)(2,1)}, u32[]{:S(2)}, u32[]{:S(2)}) async-start(bf16[32,40,1792]{2,1,0:T(8,128)(2,1)} %bitcast.58), calls=%async_computation.6 | async-start | bytes 9175040 | tf_op jit(solution)/shard_map/all_to_all | solution.py:330
  215.7 20.6 %shard_map.132.w_ref = bf16[4,1792,512]{2,1,0:T(8,128)(2,1)} custom-call(bf16[1792,2,1024]{2,1,0:T(2,128)(2,1)} %bitcast.61, f32[1792,1]{1,0:T(8,128)} %broadcast_in_dim.137.g_ref), custom_call_target="tpu_custom_call" | custom-call | flops 3670016 | bytes 14680064 | tf_op jit(solution)/shard_map/pallas_call | solution.py:170
  236.9 44.7 %all-to-all-done.6 = bf16[32,40,1792]{2,1,0:T(8,128)(2,1)} async-done(((bf16[32,40,1792]{2,1,0:T(8,128)(2,1)}), bf16[32,40,1792]{2,1,0:T(8,128)(2,1)}, u32[]{:S(2)}, u32[]{:S(2)}) %all-to-all-start.6) | async-done | bytes 4587552 | tf_op jit(solution)/shard_map/all_to_all | solution.py:330
  281.5 9.7 %shard_map.133 = bf16[2,1280,512]{2,1,0:T(8,128)(2,1)} custom-call(s32[2]{0:T(128)} %pad_add_fusion.1.idx, bf16[1280,1792]{1,0:T(8,128)(2,1)} %bitcast.17.x_ref, bf16[4,1792,512]{2,1,0:T(8,128)(2,1)} %shard_map.132.w_ref), custom_call_target="tpu_custom_call" | custom-call | flops 4697620480 | bytes 8257536 | tf_op jit(solution)/shard_map/pallas_call | solution.py:191
  292.9 9.7 %shard_map.134 = bf16[2,1280,512]{2,1,0:T(8,128)(2,1)} custom-call(s32[2]{0:T(128)} %pad_add_fusion.2.idx, bf16[1280,1792]{1,0:T(8,128)(2,1)} %bitcast.17.x_ref, bf16[4,1792,512]{2,1,0:T(8,128)(2,1)} %shard_map.132.w_ref), custom_call_target="tpu_custom_call" | custom-call | flops 4697620480 | bytes 8257536 | tf_op jit(solution)/shard_map/pallas_call | solution.py:191
  308.9 29.5 %all_to_all.60 = f32[4,1,128]{2,1,0:T(1,128)S(1)} all-to-all(f32[4,1,128]{2,1,0:T(1,128)S(1)} %broadcast_in_dim.133), channel_id=1, replica_groups=mesh['tp'=4,'ep_0'=4,'ep_1'=4,'ep_2'=2] {'tp'}, dimensions={0} | all-to-all | bytes 4096 | tf_op jit(solution)/shard_map/all_to_all | solution.py:30
  339.3 12.9 %all-to-all-start.8 = ((f32[32,1,128]{2,1,0:T(1,128)}), f32[32,1,128]{2,1,0:T(1,128)S(1)}, u32[]{:S(2)}, u32[]{:S(2)}) async-start(f32[32,1,128]{2,1,0:T(1,128)} %bitcast.22), calls=%async_computation.8 | async-start | bytes 32768 | tf_op jit(solution)/shard_map/all_to_all | solution.py:339
  362.5 11.9 %collective-permute-done.9.refs_2_ = bf16[1280,256]{1,0:T(8,128)(2,1)S(1)} collective-permute-done((bf16[1280,256]{1,0:T(8,128)(2,1)S(1)}, bf16[1280,256]{1,0:T(8,128)(2,1)S(1)}, u32[]{:S(2)}, u32[]{:S(2)}) %collective-permute-start.9) | collective-permute-done | bytes 655392 | tf_op jit(solution)/shard_map/ppermute | solution.py:25
  376.9 20.6 %shard_map.136.w_ref = bf16[4,1792,512]{2,1,0:T(8,128)(2,1)} custom-call(bf16[1792,2,1024]{2,1,0:T(2,128)(2,1)} %all-gather.5.cloned.1.call-done.w_ref, f32[1792,1]{1,0:T(8,128)} %broadcast_in_dim.137.g_ref), custom_call_target="tpu_custom_call" | custom-call | flops 3670016 | bytes 14680064 | tf_op jit(solution)/shard_map/pallas_call | solution.py:170
  398.1 6.0 %shard_map.137 = bf16[4,128,512]{2,1,0:T(8,128)(2,1)} custom-call(s32[4]{0:T(128)} %iota.47.idx, bf16[128,1792]{1,0:T(8,128)(2,1)} %copy-done, bf16[4,1792,512]{2,1,0:T(8,128)(2,1)} %shard_map.136.w_ref), custom_call_target="tpu_custom_call" | custom-call | flops 939524096 | bytes 7798784 | tf_op jit(solution)/shard_map/pallas_call | solution.py:191
  410.3 11.2 %shard_map.135 = bf16[1280,1792]{1,0:T(8,128)(2,1)} custom-call(s32[4]{0:T(128)} %pad_add_fusion.idx, bf16[1280,256]{1,0:T(8,128)(2,1)} %copy-done.3, bf16[1280,256]{1,0:T(8,128)(2,1)} %copy-done.6, bf16[1280,256]{1,0:T(8,128)(2,1)} %copy-done.5, bf16[1280,256]{1,0:T(8,128)(2,1)} %copy-done.7, bf16[1024,1792]{1,0:T(8,128)(2,1)} %bitcast.54, ...), custom_call_target="tpu_custom_call" | custom-call | flops 4697620480 | bytes 4587520 | tf_op jit(solution)/shard_map/pallas_call | solution.py:224
  421.5 10.9 %all-to-all-start.9 = ((bf16[32,40,1792]{2,1,0:T(8,128)(2,1)}), bf16[32,40,1792]{2,1,0:T(8,128)(2,1)}, u32[]{:S(2)}, u32[]{:S(2)}) async-start(bf16[32,40,1792]{2,1,0:T(8,128)(2,1)} %bitcast.59), calls=%async_computation.9 | async-start | bytes 9175040 | tf_op jit(solution)/shard_map/all_to_all | solution.py:360
  432.8 68.6 %all-to-all-done.9 = bf16[32,40,1792]{2,1,0:T(8,128)(2,1)} async-done(((bf16[32,40,1792]{2,1,0:T(8,128)(2,1)}), bf16[32,40,1792]{2,1,0:T(8,128)(2,1)}, u32[]{:S(2)}, u32[]{:S(2)}) %all-to-all-start.9) | async-done | bytes 4587552 | tf_op jit(solution)/shard_map/all_to_all | solution.py:360
  (132 shorter events, 92.6 us)
Async XLA Ops:
  6.5 103.4 %all-gather.9.cloned.1.call-start = ((), (), s32[]{:S(2)}) async-start(), calls=%async_computation.14 | async-start | bytes 8028160 | tf_op jit(solution)/shard_map/all_gather | solution.py:292
  20.1 9.4 %all-to-all-start.3 = ((s32[8,8,128]{2,1,0:T(8,128)}), s32[8,8,128]{2,1,0:T(8,128)S(1)}, u32[]{:S(2)}, u32[]{:S(2)}) async-start(s32[8,8,128]{2,1,0:T(8,128)} %broadcast_in_dim_broadcast_in_dim_broadcast_in_dim.2), calls=%async_computation.3 | async-start | bytes 65536 | tf_op jit(solution)/shard_map/all_to_all | solution.py:30
  30.3 14.0 %all-to-all-start = ((s32[32,8,128]{2,1,0:T(8,128)}), s32[32,8,128]{2,1,0:T(8,128)S(1)}, u32[]{:S(2)}, u32[]{:S(2)}) async-start(s32[32,8,128]{2,1,0:T(8,128)} %broadcast_in_dim.120), calls=%async_computation | async-start | bytes 262144 | tf_op jit(solution)/shard_map/all_to_all | solution.py:279
  44.3 15.6 %all-to-all-start.4 = ((bf16[8,128,224]{1,2,0:T(8,128)(2,1)}), bf16[8,128,224]{1,2,0:T(8,128)(2,1)S(1)}, u32[]{:S(2)}, u32[]{:S(2)}) async-start(bf16[8,128,224]{1,2,0:T(8,128)(2,1)} %copy.38), calls=%async_computation.4 | async-start | bytes 917504 | tf_op jit(solution)/shard_map/all_to_all | solution.py:302
  59.9 26.3 %all-to-all-start.2 = ((bf16[32,64,224]{2,1,0:T(8,128)(2,1)}), bf16[32,64,224]{2,1,0:T(8,128)(2,1)S(1)}, u32[]{:S(2)}, u32[]{:S(2)}) async-start(bf16[32,64,224]{2,1,0:T(8,128)(2,1)} %bitcast.62), calls=%async_computation.2 | async-start | bytes 2097152 | tf_op jit(solution)/shard_map/all_to_all | solution.py:309
  69.2 307.7 %all-gather.5.cloned.1.call-start = ((), (), s32[]{:S(2)}) async-start(), calls=%async_computation.12 | async-start | bytes 7569408 | tf_op jit(solution)/shard_map/all_gather | solution.py:293
  69.4 26.9 %collective-permute-start.4 = (bf16[1024,224]{1,0:T(8,128)(2,1)S(1)}, bf16[1024,224]{1,0:T(8,128)(2,1)S(1)}, u32[]{:S(2)}, u32[]{:S(2)}) collective-permute-start(bf16[1024,224]{1,0:T(8,128)(2,1)S(1)} %bitcast.66), channel_id=1, source_target_pairs={{0,64},{32,96},{64,0},{96,32},{1,65},{33,97},{65,1},{97,33},{2,66}... | collective-permute-start | bytes 1376264 | tf_op jit(solution)/shard_map/ppermute | solution.py:25
  93.0 12.3 %collective-permute-start.1 = (bf16[1024,224]{1,0:T(8,128)(2,1)}, bf16[1024,224]{1,0:T(8,128)(2,1)S(1)}, u32[]{:S(2)}, u32[]{:S(2)}) collective-permute-start(bf16[1024,224]{1,0:T(8,128)(2,1)} %bitcast.63), channel_id=1, source_target_pairs={{0,64},{32,96},{64,0},{96,32},{1,65},{33,97},{65,1},{97,33},{2,66}... | collective-permute-start | bytes 1376264 | tf_op jit(solution)/shard_map/ppermute | solution.py:25
  94.2 15.7 %collective-permute-start.3 = (bf16[1024,224]{1,0:T(8,128)(2,1)S(1)}, bf16[1024,224]{1,0:T(8,128)(2,1)S(1)}, u32[]{:S(2)}, u32[]{:S(2)}) collective-permute-start(bf16[1024,224]{1,0:T(8,128)(2,1)S(1)} %bitcast.67), channel_id=1, source_target_pairs={{0,32},{32,0},{64,96},{96,64},{1,33},{33,1},{65,97},{97,65},{2,34}... | collective-permute-start | bytes 1376264 | tf_op jit(solution)/shard_map/ppermute | solution.py:25
  96.3 13.5 %collective-permute-start.5 = (bf16[1024,224]{1,0:T(8,128)(2,1)S(1)}, bf16[1024,224]{1,0:T(8,128)(2,1)}, u32[]{:S(2)}, u32[]{:S(2)}) collective-permute-start(bf16[1024,224]{1,0:T(8,128)(2,1)S(1)} %collective-permute-done.4.refs_2_), channel_id=1, source_target_pairs={{0,32},{32,0},{64,96},{96,64},{1,33},{33,1},{65,97},{97,65},{2,34}... | collective-permute-start | bytes 1376264 | tf_op jit(solution)/shard_map/ppermute | solution.py:25
  96.4 25.0 %collective-permute-start = (bf16[1024,224]{1,0:T(8,128)(2,1)}, bf16[1024,224]{1,0:T(8,128)(2,1)S(1)}, u32[]{:S(2)}, u32[]{:S(2)}) collective-permute-start(bf16[1024,224]{1,0:T(8,128)(2,1)} %bitcast.64), channel_id=1, source_target_pairs={{0,32},{32,0},{64,96},{96,64},{1,33},{33,1},{65,97},{97,65},{2,34}... | collective-permute-start | bytes 1376264 | tf_op jit(solution)/shard_map/ppermute | solution.py:25
  105.3 16.1 %collective-permute-start.2 = (bf16[1024,224]{1,0:T(8,128)(2,1)S(1)}, bf16[1024,224]{1,0:T(8,128)(2,1)S(1)}, u32[]{:S(2)}, u32[]{:S(2)}) collective-permute-start(bf16[1024,224]{1,0:T(8,128)(2,1)S(1)} %collective-permute-done.1.refs_2_), channel_id=1, source_target_pairs={{0,32},{32,0},{64,96},{96,64},{1,33},{33,1},{65,97},{97,65},{2,34}... | collective-permute-start | bytes 1376264 | tf_op jit(solution)/shard_map/ppermute | solution.py:25
  134.8 65.1 %all-to-all-start.5 = ((bf16[8,128,1792]{2,1,0:T(8,128)(2,1)}), bf16[8,128,1792]{2,1,0:T(8,128)(2,1)}, u32[]{:S(2)}, u32[]{:S(2)}) async-start(bf16[8,128,1792]{2,1,0:T(8,128)(2,1)} %bitcast.60), calls=%async_computation.5 | async-start | bytes 7340032 | tf_op jit(solution)/shard_map/all_to_all | solution.py:324
  206.0 75.5 %all-to-all-start.6 = ((bf16[32,40,1792]{2,1,0:T(8,128)(2,1)}), bf16[32,40,1792]{2,1,0:T(8,128)(2,1)}, u32[]{:S(2)}, u32[]{:S(2)}) async-start(bf16[32,40,1792]{2,1,0:T(8,128)(2,1)} %bitcast.58), calls=%async_computation.6 | async-start | bytes 9175040 | tf_op jit(solution)/shard_map/all_to_all | solution.py:330
  291.3 11.4 %collective-permute-start.6 = (bf16[2,1280,512]{2,1,0:T(8,128)(2,1)}, bf16[2,1280,512]{2,1,0:T(8,128)(2,1)S(1)}, u32[]{:S(2)}, u32[]{:S(2)}) collective-permute-start(bf16[2,1280,512]{2,1,0:T(8,128)(2,1)} %shard_map.133), channel_id=1, source_target_pairs={{0,32},{32,0},{64,96},{96,64},{1,33},{33,1},{65,97},{97,65},{2,34}... | collective-permute-start | bytes 7864328 | tf_op jit(solution)/shard_map/ppermute | solution.py:25
  305.4 50.8 %collective-permute-start.7 = (bf16[1280,512]{1,0:T(8,128)(2,1)}, bf16[1280,512]{1,0:T(8,128)(2,1)}, u32[]{:S(2)}, u32[]{:S(2)}) collective-permute-start(bf16[1280,512]{1,0:T(8,128)(2,1)} %fusion.3), channel_id=1, source_target_pairs={{0,64},{32,96},{64,0},{96,32},{1,65},{33,97},{65,1},{97,33},{2,66}... | collective-permute-start | bytes 3932168 | tf_op jit(solution)/shard_map/ppermute | solution.py:25
  339.3 16.8 %all-to-all-start.8 = ((f32[32,1,128]{2,1,0:T(1,128)}), f32[32,1,128]{2,1,0:T(1,128)S(1)}, u32[]{:S(2)}, u32[]{:S(2)}) async-start(f32[32,1,128]{2,1,0:T(1,128)} %bitcast.22), calls=%async_computation.8 | async-start | bytes 32768 | tf_op jit(solution)/shard_map/all_to_all | solution.py:339
  352.2 156.7 %all-gather.7.cloned.1.call-start = ((), (), s32[]{:S(2)}) async-start(), calls=%async_computation.13 | async-start | bytes 3784704 | tf_op jit(solution)/shard_map/all_gather | solution.py:294
  358.9 15.5 %collective-permute-start.9 = (bf16[1280,256]{1,0:T(8,128)(2,1)S(1)}, bf16[1280,256]{1,0:T(8,128)(2,1)S(1)}, u32[]{:S(2)}, u32[]{:S(2)}) collective-permute-start(bf16[1280,256]{1,0:T(8,128)(2,1)S(1)} %fusion.4.refs_0_), channel_id=1, source_target_pairs={{0,64},{32,96},{64,0},{96,32},{1,65},{33,97},{65,1},{97,33},{2,66}... | collective-permute-start | bytes 1966088 | tf_op jit(solution)/shard_map/ppermute | solution.py:25
  360.4 48.8 %collective-permute-start.8 = (bf16[1280,256]{1,0:T(8,128)(2,1)S(1)}, bf16[1280,256]{1,0:T(8,128)(2,1)S(1)}, u32[]{:S(2)}, u32[]{:S(2)}) collective-permute-start(bf16[1280,256]{1,0:T(8,128)(2,1)S(1)} %fusion.4.refs_0_), channel_id=1, source_target_pairs={{0,32},{32,0},{64,96},{96,64},{1,33},{33,1},{65,97},{97,65},{2,34}... | collective-permute-start | bytes 1966088 | tf_op jit(solution)/shard_map/ppermute | solution.py:25
  374.3 34.9 %collective-permute-start.10 = (bf16[1280,256]{1,0:T(8,128)(2,1)S(1)}, bf16[1280,256]{1,0:T(8,128)(2,1)S(1)}, u32[]{:S(2)}, u32[]{:S(2)}) collective-permute-start(bf16[1280,256]{1,0:T(8,128)(2,1)S(1)} %collective-permute-done.9.refs_2_), channel_id=1, source_target_pairs={{0,32},{32,0},{64,96},{96,64},{1,33},{33,1},{65,97},{97,65},{2,34}... | collective-permute-start | bytes 1966088 | tf_op jit(solution)/shard_map/ppermute | solution.py:25
  404.2 17.3 %all-to-all-start.10 = ((bf16[4,128,512]{2,1,0:T(8,128)(2,1)}), bf16[4,128,512]{2,1,0:T(8,128)(2,1)S(1)}, u32[]{:S(2)}, u32[]{:S(2)}) async-start(bf16[4,128,512]{2,1,0:T(8,128)(2,1)} %shard_map.137), calls=%async_computation.10 | async-start | bytes 1048576 | tf_op jit(solution)/shard_map/all_to_all | solution.py:366
  421.5 79.9 %all-to-all-start.9 = ((bf16[32,40,1792]{2,1,0:T(8,128)(2,1)}), bf16[32,40,1792]{2,1,0:T(8,128)(2,1)}, u32[]{:S(2)}, u32[]{:S(2)}) async-start(bf16[32,40,1792]{2,1,0:T(8,128)(2,1)} %bitcast.59), calls=%async_computation.9 | async-start | bytes 9175040 | tf_op jit(solution)/shard_map/all_to_all | solution.py:360
  502.2 7.8 %all-to-all-start.11 = ((bf16[4,128,256]{1,2,0:T(8,128)(2,1)}), bf16[4,128,256]{1,2,0:T(8,128)(2,1)S(1)}, u32[]{:S(2)}, u32[]{:S(2)}) async-start(bf16[4,128,256]{1,2,0:T(8,128)(2,1)} %broadcast_in_dim.136), calls=%async_computation.11 | async-start | bytes 524288 | tf_op jit(solution)/shard_map/all_to_all | solution.py:30
  (20 other events, 396.8 us)
Sparse Core Ops, SparseCore 0:
  9.0 80.0 all-gather.8
  92.0 129.5 all-gather.4
  356.0 88.5 all-gather.6
